TPU v7x, 32 devices: a whole 2x2x4 slice. The times are simulated.
32 devices in a mesh: groups: 2 (over y), row: 8 (over z, x), col: 2 (over core).
Axes of the slice: x: 2, y: 2, z: 4, core: 2. Of those that a mesh axis runs over, the one named last changes fastest.
Arguments:
- gram_old: bfloat16 [28672, 14336], P(('groups', 'row'), 'col'), parts along dimension 0, may hold values from -10 to 256, as said below
- activations: bfloat16 [256, 14336], P('groups', 'row'), parts along dimension 0, may hold values from -0.5 to 0.5
- weights: float32 [14336, 512], P('row', ('groups', 'col')), parts along dimension 1, may hold values from -6 to 6
- block_mask: int32 [112, 4], P(None, 'groups'), parts along dimension 1, may hold values 0 or 1
Outputs:
- pruned: float32 [14336, 512], P('row', ('groups', 'col')), parts along dimension 1
There are 2 independent parts, one for each index of `groups`. A program takes and returns all parts, laid end to end along the dimension named above; each array names one. Nothing has to cross between parts.
Inputs may be any that keep to these rules, and one draw needn't show every extreme that they name: `gram_old`: symmetric and positive definite.
All inputs are finite; a program needn't handle non-finite values.
Results may differ from a plain program's by a relative error of at most 0.00076.
Values may be sent and summed in bfloat16 or wider, within the bound.
A program may use at most 128 MiB of HBM per device.

v0:
```python
import jax
import jax.numpy as jnp
from jax import lax
from jax.sharding import PartitionSpec as P

K = 14336
BLK = 128
damping_ratio = 0.3
epsilon = 1e-06


def partner(value, axis, distance):
    return lax.ppermute(value, axis, [(i, i ^ 1 << distance) for i in range(lax.axis_size(axis))])


def expand_local(block_mask, row_offset, row_count, col_offset, col_count):
    row_ids = (row_offset + jnp.arange(row_count, dtype=jnp.int32)) // BLK
    col_ids = (col_offset + jnp.arange(col_count, dtype=jnp.int32)) // BLK
    pick_rows = (
        row_ids[:, None] == jnp.arange(block_mask.shape[0], dtype=jnp.int32)[None, :]
    ).astype(jnp.float32)
    pick_cols = (
        col_ids[:, None] == jnp.arange(block_mask.shape[1], dtype=jnp.int32)[None, :]
    ).astype(jnp.float32)
    partial_rows = jnp.dot(
        pick_rows, block_mask.astype(jnp.float32), precision=lax.Precision.HIGHEST
    )
    return jnp.dot(partial_rows, pick_cols.T, precision=lax.Precision.HIGHEST)


def update_product(activations, inner):
    high = inner.astype(jnp.bfloat16)
    low = (inner - high.astype(jnp.float32)).astype(jnp.bfloat16)
    contract = (((0,), (0,)), ((), ()))
    return lax.dot_general(
        activations, high, contract, preferred_element_type=jnp.float32
    ) + lax.dot_general(activations, low, contract, preferred_element_type=jnp.float32)


def per_device(gram_old, activations, weights, block_mask):
    row_block = gram_old.shape[0]
    half_width = gram_old.shape[1]
    width_cols = weights.shape[1]
    row_index = lax.axis_index("row")
    col_index = lax.axis_index("col")
    row_offset = row_index * row_block
    half_offset = col_index * half_width
    diag_column = row_offset + jnp.arange(row_block, dtype=jnp.int32) - half_offset
    on_diagonal = jnp.arange(half_width, dtype=jnp.int32)[None, :] == diag_column[:, None]
    trace_part = jnp.sum(jnp.where(on_diagonal, gram_old.astype(jnp.float32), 0.0))
    acts_wide = activations.astype(jnp.float32)
    trace_part = trace_part + jnp.sum(acts_wide * acts_wide) / lax.axis_size("col")
    mask_local = expand_local(block_mask, row_offset, row_block, col_index * width_cols, width_cols)

    def apply_gram(panel):
        panel_low = panel.astype(jnp.bfloat16)
        inner = lax.psum(jnp.dot(activations, panel_low, preferred_element_type=jnp.float32), "row")
        low_rank = update_product(activations, inner)
        column_panel = lax.all_gather(panel_low, "row", axis=0, tiled=True)
        own_half = lax.dynamic_slice_in_dim(column_panel, half_offset, half_width, 0)
        partner_need = lax.dynamic_slice_in_dim(
            column_panel, (1 - col_index) * half_width, half_width, 0
        )
        partner_half = partner(partner_need, "col", 0)
        own_part = jnp.dot(gram_old, own_half, preferred_element_type=jnp.float32)
        partner_part = jnp.dot(gram_old, partner_half, preferred_element_type=jnp.float32)
        return own_part + partner(partner_part, "col", 0) + low_rank

    kept_weights = mask_local * weights
    pruned_diff = kept_weights - weights
    grad_first = apply_gram(pruned_diff)
    step_dir = mask_local * grad_first
    curvature = apply_gram(step_dir)
    masked_curve = mask_local * curvature
    local_square = jnp.sum(step_dir * step_dir)
    local_curve = jnp.sum(step_dir * curvature)
    local_curve_square = jnp.sum(masked_curve * masked_curve)
    grad_square, grad_curve, curve_square, trace_total = lax.psum(
        jnp.stack([local_square, local_curve, local_curve_square, trace_part]), ("row", "col")
    )
    damping = damping_ratio * trace_total / K
    step_first = grad_square / (grad_curve + damping * grad_square + epsilon)
    step_second = (grad_curve + damping * grad_square) / (
        curve_square + 2.0 * damping * grad_curve + damping * damping * grad_square + epsilon
    )
    grad_second = grad_first - step_first * curvature
    return kept_weights - step_first * step_dir - step_second * (mask_local * grad_second)


def solution(mesh):
    placed = (
        P(("groups", "row"), "col"),
        P("groups", "row"),
        P("row", ("groups", "col")),
        P(None, "groups"),
    )
    return jax.shard_map(
        per_device,
        mesh=mesh,
        in_specs=placed,
        out_specs=P("row", ("groups", "col")),
        check_vma=False,
    )
```

profile of v0, /device:TPU:0, one launch (start us, length us, event | category | flops | bytes accessed | tf_op | source)
XLA Modules:
  0.0 419.9 jit_solution(6358814029816759565)
XLA Ops:
  6.6 2.0 fusion.4
  8.6 2.9 subtract_convert_fusion
  11.6 0.0 all-gather.3.cloned.1.call-update
  11.6 0.0 all-reduce.3.cloned.1.call-start
  11.6 69.0 %all-gather.3.cloned.1.call-done = bf16[14336,128]{1,0:T(8,128)(2,1)} async-done(((bf16[1792,128]{1,0:T(8,128)(2,1)}), bf16[14336,128]{1,0:T(8,128)(2,1)}) %all-gather.3.cloned.1.call-update) | async-done | bytes 3670032 | tf_op jit(solution)/shard_map/all_gather | solution.py:59
  80.7 2.9 constant_dynamic-slice_fusion.1
  83.5 0.9 convolution_bitcast_fusion.5
  84.5 0.0 all-reduce.3.cloned.1.call-update
  84.5 0.0 all-gather.5.cloned.1.call-start
  84.6 68.2 %all-reduce.3.cloned.1.call-done = f32[128,128]{0,1:T(8,128)} async-done(((f32[128,128]{0,1:T(8,128)}), f32[128,128]{0,1:T(8,128)}) %all-reduce.3.cloned.1.call-update) | async-done | bytes 65552 | tf_op jit(solution)/shard_map/psum | solution.py:57
  152.8 1.2 fusion.12
  154.0 12.5 %convolution_bitcast_fusion.2 = f32[1792,128]{1,0:T(8,128)S(1)} fusion(bf16[1792,7168]{1,0:T(8,128)(2,1)} %param.4, bf16[7168,128]{1,0:T(8,128)(2,1)} %collective-permute-done), kind=kOutput, calls=%fused_computation.6 | convolution fusion | flops 3288334336 | bytes 28442624 | tf_op jit(solution)/shard_map/dot_general | solution.py:66
  166.5 0.1 collective-permute-start.1
  166.5 11.8 %convolution_bitcast_fusion.3 = f32[1792,128]{1,0:T(8,128)S(1)} fusion(bf16[1792,7168]{1,0:T(8,128)(2,1)} %param.4, bf16[14336,128]{1,0:T(8,128)(2,1)S(1)} %copy-done.4, s32[]{:T(128)S(6)} %select_n.32), kind=kOutput, calls=%fused_computation.7 | convolution fusion | flops 3288334336 | bytes 28442628 | tf_op jit(solution)/shard_map/dot_general | solution.py:65
  178.4 1.8 fusion.24
  180.2 0.2 all-reduce.5.cloned.1.call-start
  180.5 66.2 %all-gather.5.cloned.1.call-done = bf16[14336,128]{1,0:T(8,128)(2,1)} async-done(((bf16[1792,128]{1,0:T(8,128)(2,1)}), bf16[14336,128]{1,0:T(8,128)(2,1)}) %all-gather.5.cloned.1.call-update) | async-done | bytes 3670032 | tf_op jit(solution)/shard_map/all_gather | solution.py:59
  246.7 1.6 constant_dynamic-slice_fusion
  248.3 0.1 collective-permute-start.2
  248.4 23.6 %select_reduce_fusion = f32[]{:T(128)} fusion(bf16[1792,7168]{1,0:T(8,128)(2,1)} %param.4, s32[1792]{0:T(1024)S(1)} %get-tuple-element.20), kind=kLoop, calls=%fused_computation | loop fusion | flops 51380224 | bytes 25697284 | tf_op jit(solution)/shard_map/reduce_sum | solution.py:50
  272.0 12.8 %convolution_bitcast_fusion = f32[1792,128]{1,0:T(8,128)} fusion(bf16[1792,7168]{1,0:T(8,128)(2,1)} %param.4, bf16[7168,128]{1,0:T(8,128)(2,1)S(1)} %collective-permute-done.2), kind=kOutput, calls=%fused_computation.4 | convolution fusion | flops 3288334336 | bytes 28442624 | tf_op jit(solution)/shard_map/dot_general | solution.py:66
  284.8 0.5 collective-permute-start.3
  285.3 1.0 convolution_bitcast_fusion.4
  286.3 0.8 multiply_reduce_fusion
  288.3 66.2 %all-reduce.5.cloned.1.call-done = f32[128,128]{0,1:T(8,128)} async-done(((f32[128,128]{0,1:T(8,128)}), f32[128,128]{0,1:T(8,128)}) %all-reduce.5.cloned.1.call-update) | async-done | bytes 65552 | tf_op jit(solution)/shard_map/psum | solution.py:57
  354.5 1.2 fusion.9
  355.7 1.2 fusion.1
  357.0 14.0 %multiply_reduce_fusion.3 = (f32[]{:T(128)}, f32[]{:T(128)}, f32[]{:T(128)}, f32[1792,128]{1,0:T(8,128)}) fusion(f32[1792,128]{1,0:T(8,128)S(1)} %copy-done.3, f32[1792,128]{1,0:T(8,128)S(1)} %get-tuple-element.16, f32[1792,128]{1,0:T(8,128)S(1)} %fusion.1, f32[1792,128]{1,0:T(8,128)} %collective-permute-done.3, bf16[1792,7168]{1,0:T(8,128)(2,1)} %param.4, ...), kind=kOutput, calls=%fused_computation.19 | convolution fusion | flops 3290398720 | bytes 32112656 | tf_op jit(solution)/shard_map/dot_general | solution.py:65
  371.0 2.0 pad_maximum_fusion
  373.0 30.3 %psum.23 = f32[4]{0:T(128)S(1)} all-reduce(f32[4]{0:T(128)S(1)} %pad_maximum_fusion), channel_id=1, replica_groups=mesh['groups'=2,'row'=8,'col'=2] {'row','col'}, use_global_device_ids=true, to_apply=%region_7.8 | all-reduce | flops 4 | bytes 32 | tf_op jit(solution)/shard_map/psum | solution.py:78
  403.2 0.6 fusion.26
  410.2 3.2 multiply_subtract_fusion
  (22 shorter events, 0.1 us)
Async XLA Ops:
  6.5 74.1 %all-gather.3.cloned.1.call-start = ((), (), s32[]{:S(2)}) async-start(), calls=%async_computation | async-start | bytes 4128768 | tf_op jit(solution)/shard_map/all_gather | solution.py:59
  8.6 74.9 %copy-start = (bf16[128,1792]{1,0:T(8,128)(2,1)S(1)}, bf16[128,1792]{1,0:T(8,128)(2,1)}, u32[]{:S(2)}) copy-start(bf16[128,1792]{1,0:T(8,128)(2,1)} %param.5) | copy-start | bytes 1376260
  11.6 72.0 %copy-start.2 = (bf16[1792,128]{1,0:T(8,128)(2,1)S(1)}, bf16[1792,128]{1,0:T(8,128)(2,1)}, u32[]{:S(2)}) copy-start(bf16[1792,128]{1,0:T(8,128)(2,1)} %get-tuple-element.10) | copy-start | bytes 1376260
  11.6 141.2 %all-reduce.3.cloned.1.call-start = ((), (), s32[]{:S(2)}) async-start(), calls=%async_computation.1 | async-start | bytes 131072 | tf_op jit(solution)/shard_map/psum | solution.py:57
  83.5 70.4 %collective-permute-start = (bf16[7168,128]{1,0:T(8,128)(2,1)}, bf16[7168,128]{1,0:T(8,128)(2,1)}, u32[]{:S(2)}, u32[]{:S(2)}) collective-permute-start(bf16[7168,128]{1,0:T(8,128)(2,1)} %constant_dynamic-slice_fusion.1), channel_id=1, source_target_pairs={{0,1},{1,0},{2,3},{3,2},{4,5},{5,4},{6,7},{7,6},{8,9},{9,8},{10,11... | collective-permute-start | bytes 5505032 | tf_op jit(solution)/shard_map/ppermute | solution.py:13
  84.5 162.2 %all-gather.5.cloned.1.call-start = ((), (), s32[]{:S(2)}) async-start(), calls=%async_computation.2 | async-start | bytes 4128768 | tf_op jit(solution)/shard_map/all_gather | solution.py:59
  153.9 12.6 %copy-start.4 = (bf16[14336,128]{1,0:T(8,128)(2,1)S(1)}, bf16[14336,128]{1,0:T(8,128)(2,1)}, u32[]{:S(2)}) copy-start(bf16[14336,128]{1,0:T(8,128)(2,1)} %all-gather.3.cloned.1.call-done) | copy-start | bytes 11010052
  166.4 11.9 %copy-start.5 = (f32[128,128]{0,1:T(8,128)S(1)}, f32[128,128]{0,1:T(8,128)}, u32[]{:S(2)}) copy-start(f32[128,128]{0,1:T(8,128)} %all-reduce.3.cloned.1.call-done) | copy-start | bytes 196612
  166.5 11.9 %collective-permute-start.1 = (f32[1792,128]{1,0:T(8,128)S(1)}, f32[1792,128]{1,0:T(8,128)S(1)}, u32[]{:S(2)}, u32[]{:S(2)}) collective-permute-start(f32[1792,128]{1,0:T(8,128)S(1)} %convolution_bitcast_fusion.2), channel_id=1, source_target_pairs={{0,1},{1,0},{2,3},{3,2},{4,5},{5,4},{6,7},{7,6},{8,9},{9,8},{10,11... | collective-permute-start | bytes 2752520 | tf_op jit(solution)/shard_map/ppermute | solution.py:13
  180.2 174.2 %all-reduce.5.cloned.1.call-start = ((), (), s32[]{:S(2)}) async-start(), calls=%async_computation.3 | async-start | bytes 131072 | tf_op jit(solution)/shard_map/psum | solution.py:57
  248.3 23.7 %collective-permute-start.2 = (bf16[7168,128]{1,0:T(8,128)(2,1)S(1)}, bf16[7168,128]{1,0:T(8,128)(2,1)S(1)}, u32[]{:S(2)}, u32[]{:S(2)}) collective-permute-start(bf16[7168,128]{1,0:T(8,128)(2,1)S(1)} %constant_dynamic-slice_fusion), channel_id=1, source_target_pairs={{0,1},{1,0},{2,3},{3,2},{4,5},{5,4},{6,7},{7,6},{8,9},{9,8},{10,11... | collective-permute-start | bytes 5505032 | tf_op jit(solution)/shard_map/ppermute | solution.py:13
  272.0 13.3 %copy-start.1 = (bf16[1792,128]{1,0:T(8,128)(2,1)S(1)}, bf16[1792,128]{1,0:T(8,128)(2,1)}, u32[]{:S(2)}) copy-start(bf16[1792,128]{1,0:T(8,128)(2,1)} %get-tuple-element.8) | copy-start | bytes 1376260
  284.8 72.2 %collective-permute-start.3 = (f32[1792,128]{1,0:T(8,128)}, f32[1792,128]{1,0:T(8,128)}, u32[]{:S(2)}, u32[]{:S(2)}) collective-permute-start(f32[1792,128]{1,0:T(8,128)} %convolution_bitcast_fusion), channel_id=1, source_target_pairs={{0,1},{1,0},{2,3},{3,2},{4,5},{5,4},{6,7},{7,6},{8,9},{9,8},{10,11... | collective-permute-start | bytes 2752520 | tf_op jit(solution)/shard_map/ppermute | solution.py:13
  354.5 2.5 copy-start.3
Sparse Core Ops, SparseCore 0:
  11.7 68.9 all-gather.2
  84.6 68.1 all-reduce.2
  180.4 66.2 all-gather.4
  286.4 68.0 all-reduce.4
where the time goes:
time: 420 us
  waiting for transfers between devices  270 us (64%)
  matrix products  63.5 us (15%)
  blocking collectives  30.3 us (7%)
  other arithmetic  29.6 us (7%)
  between operations  20.8 us (5%)
  local copies, waits for them, and re-layouts  5.13 us (1%)
    all_gather x2, waiting for transfers between devices, apply_gram(): column_panel = lax.all_gather(panel_low, 'row', axis=0, tiled=True)  135 us
    psum x2, waiting for transfers between devices, apply_gram(): lax.psum(jnp.dot(activations, panel_low, preferred_element_type=jnp.float...  134 us
    psum x1, blocking collectives, per_device(): lax.psum(jnp.stack([local_square, local_curve, local_curve_square, trace_...  30.3 us
    dot_general x2, matrix products, apply_gram(): own_part = jnp.dot(gram_old, own_half, preferred_element_type=jnp.float32)  25.8 us
    dot_general x2, matrix products, apply_gram(): jnp.dot(gram_old, partner_half, preferred_element_type=jnp.float32)  25.3 us
    reduce_sum x1, other arithmetic, per_device(): jnp.sum(jnp.where(on_diagonal, gram_old.astype(jnp.float32), 0.0))  23.6 us
  transfers between devices with their start and end apart: 8, of which 4 were waited for; matrix products, arithmetic and copies ran while one was open for 10% of the time, Pallas kernels for 0%

commit v1 on v0

--- a/solution.py
+++ b/solution.py
@@ -56,7 +56,26 @@
         panel_low = panel.astype(jnp.bfloat16)
         inner = lax.psum(jnp.dot(activations, panel_low, preferred_element_type=jnp.float32), "row")
         low_rank = update_product(activations, inner)
-        column_panel = lax.all_gather(panel_low, "row", axis=0, tiled=True)
+        peers, index, extent = (lax.axis_size("row"), lax.axis_index("row"), panel_low.shape[0])
+        forward = [(i_2, (i_2 + 1) % peers) for i_2 in range(peers)]
+        left = [(i_2, (i_2 - 1) % peers) for i_2 in range(peers)]
+        filled = jnp.zeros(
+            (*panel_low.shape[:0], peers * extent, *panel_low.shape[0 + 1 :]), panel_low.dtype
+        )
+        filled = lax.dynamic_update_slice_in_dim(filled, panel_low, index * extent, axis=0)
+        from_left = from_right = panel_low
+        halfway = peers // 2
+        for lap in range(1, halfway + 1):
+            from_left = lax.ppermute(from_left, "row", forward)
+            filled = lax.dynamic_update_slice_in_dim(
+                filled, from_left, (index - lap) % peers * extent, axis=0
+            )
+            if lap < peers - halfway:
+                from_right = lax.ppermute(from_right, "row", left)
+                filled = lax.dynamic_update_slice_in_dim(
+                    filled, from_right, (index + lap) % peers * extent, axis=0
+                )
+        column_panel = filled
         own_half = lax.dynamic_slice_in_dim(column_panel, half_offset, half_width, 0)
         partner_need = lax.dynamic_slice_in_dim(
             column_panel, (1 - col_index) * half_width, half_width, 0

time: 420 us -> 450 us (1.071)
  starting transfers between devices: 0.94 us -> 23.6 us
  local copies, waits for them, and re-layouts: 5.13 us -> 12 us
    all_gather x2 -> x0, waiting for transfers between devices: 135 us -> none  [apply_gram(): column_panel = lax.all_gather(panel_low, 'row', axis=0, tiled=True)]
    ppermute x0 -> x14, waiting for transfers between devices: none -> 133 us  [the longest x8 79.3 us: apply_gram(): from_left = lax.ppermute(from_left, 'row', forward)]
    ppermute x0 -> x14, starting transfers between devices: none -> 23.3 us  [the longest x6 15.9 us: apply_gram(): from_right = lax.ppermute(from_right, 'row', left)]
    dynamic_update_slice x0 -> x14, local copies, waits for them, and re-layouts: none -> 6.12 us  [the longest x8 3.5 us: apply_gram(): lax.dynamic_update_slice_in_dim(filled, from_left, (index - lap) % peers...]
  transfers between devices with their start and end apart: 8 -> 20, of which waited for: 4 -> 13; matrix products, arithmetic and copies ran while one was open for 10% -> 8% of each run, Pallas kernels for 0% -> 0%
where the time goes in v1:
time: 450 us
  waiting for transfers between devices  270 us (60%)
  matrix products  62.8 us (14%)
  blocking collectives  30.3 us (7%)
  other arithmetic  30.1 us (7%)
  starting transfers between devices  23.6 us (5%)
  between operations  21.2 us (5%)
  local copies, waits for them, and re-layouts  12 us (3%)
    psum x2, waiting for transfers between devices, apply_gram(): lax.psum(jnp.dot(activations, panel_low, preferred_element_type=jnp.float...  133 us
    ppermute x8, waiting for transfers between devices, apply_gram(): from_left = lax.ppermute(from_left, 'row', forward)  79.3 us
    ppermute x6, waiting for transfers between devices, apply_gram(): from_right = lax.ppermute(from_right, 'row', left)  54.1 us
    psum x1, blocking collectives, per_device(): lax.psum(jnp.stack([local_square, local_curve, local_curve_square, trace_...  30.3 us
    dot_general x2, matrix products, apply_gram(): own_part = jnp.dot(gram_old, own_half, preferred_element_type=jnp.float32)  26.6 us
    dot_general x2, matrix products, apply_gram(): jnp.dot(gram_old, partner_half, preferred_element_type=jnp.float32)  25.5 us
    reduce_sum x1, other arithmetic, per_device(): jnp.sum(jnp.where(on_diagonal, gram_old.astype(jnp.float32), 0.0))  24.7 us
    ppermute x6, starting transfers between devices, apply_gram(): from_right = lax.ppermute(from_right, 'row', left)  15.9 us
  transfers between devices with their start and end apart: 20, of which 13 were waited for; matrix products, arithmetic and copies ran while one was open for 8% of the time, Pallas kernels for 0%

profile of v1, /device:TPU:0, one launch (start us, length us, event | category | flops | bytes accessed | tf_op | source)
XLA Modules:
  0.0 449.7 jit_solution(15256558612352415458)
XLA Ops:
  6.6 2.1 fusion.8
  8.7 2.0 broadcast.97.clone
  10.7 1.7 constant_dynamic-update-slice_fusion.15
  12.4 6.0 %collective-permute-start.1 = (bf16[1792,128]{1,0:T(8,128)(2,1)S(1)}, bf16[1792,128]{1,0:T(8,128)(2,1)S(1)}, u32[]{:S(2)}, u32[]{:S(2)}) collective-permute-start(bf16[1792,128]{1,0:T(8,128)(2,1)S(1)} %get-tuple-element.12), channel_id=1, source_target_pairs={{0,14},{2,0},{4,2},{6,4},{8,6},{10,8},{12,10},{14,12},{1,15},{3,1}... | collective-permute-start | bytes 1376264 | tf_op jit(solution)/shard_map/ppermute | solution.py:74
  18.5 17.3 %collective-permute-done.1 = bf16[1792,128]{1,0:T(8,128)(2,1)S(1)} collective-permute-done((bf16[1792,128]{1,0:T(8,128)(2,1)S(1)}, bf16[1792,128]{1,0:T(8,128)(2,1)S(1)}, u32[]{:S(2)}, u32[]{:S(2)}) %collective-permute-start.1) | collective-permute-done | bytes 458784 | tf_op jit(solution)/shard_map/ppermute | solution.py:74
  35.8 2.8 collective-permute-start.3
  40.2 17.0 %collective-permute-done.3 = bf16[1792,128]{1,0:T(8,128)(2,1)S(1)} collective-permute-done((bf16[1792,128]{1,0:T(8,128)(2,1)S(1)}, bf16[1792,128]{1,0:T(8,128)(2,1)S(1)}, u32[]{:S(2)}, u32[]{:S(2)}) %collective-permute-start.3) | collective-permute-done | bytes 458784 | tf_op jit(solution)/shard_map/ppermute | solution.py:74
  57.3 2.6 collective-permute-start.5
  61.5 15.3 %collective-permute-done.4 = bf16[1792,128]{1,0:T(8,128)(2,1)S(1)} collective-permute-done((bf16[1792,128]{1,0:T(8,128)(2,1)S(1)}, bf16[1792,128]{1,0:T(8,128)(2,1)S(1)}, u32[]{:S(2)}, u32[]{:S(2)}) %collective-permute-start.4) | collective-permute-done | bytes 458784 | tf_op jit(solution)/shard_map/ppermute | solution.py:69
  76.8 2.5 collective-permute-start.6
  80.9 13.6 %collective-permute-done.6 = bf16[1792,128]{1,0:T(8,128)(2,1)S(1)} collective-permute-done((bf16[1792,128]{1,0:T(8,128)(2,1)S(1)}, bf16[1792,128]{1,0:T(8,128)(2,1)S(1)}, u32[]{:S(2)}, u32[]{:S(2)}) %collective-permute-start.6) | collective-permute-done | bytes 458784 | tf_op jit(solution)/shard_map/ppermute | solution.py:69
  95.3 1.6 constant_dynamic-slice_fusion.1
  97.0 3.8 collective-permute-done.7
  100.7 12.8 %convolution_bitcast_fusion.2 = f32[1792,128]{1,0:T(8,128)} fusion(bf16[1792,7168]{1,0:T(8,128)(2,1)} %param.4, bf16[7168,128]{1,0:T(8,128)(2,1)S(1)} %collective-permute-done.7), kind=kOutput, calls=%fused_computation.6 | convolution fusion | flops 3288334336 | bytes 28442624 | tf_op jit(solution)/shard_map/dot_general | solution.py:85
  114.7 67.9 %all-reduce.3.cloned.1.call-done = f32[128,128]{0,1:T(8,128)} async-done(((f32[128,128]{0,1:T(8,128)}), f32[128,128]{0,1:T(8,128)}) %all-reduce.3.cloned.1.call-update) | async-done | bytes 65552 | tf_op jit(solution)/shard_map/psum | solution.py:57
  186.4 12.6 %constant_dynamic-update-slice_fusion.7 = (bf16[14336,128]{1,0:T(8,128)(2,1)S(1)}, bf16[1792,128]{1,0:T(8,128)(2,1)S(1)}, f32[1792,128]{1,0:T(8,128)S(1)}, f32[1792,128]{1,0:T(8,128)S(1)}) fusion(bf16[14336,128]{1,0:T(8,128)(2,1)S(1)} %broadcast.97, s32[]{:T(128)S(6)} %select_n.109, f32[1792,128]{1,0:T(8,128)S(1)} %get-tuple-element.18, ...), kind=kOutput, calls=%fused_computation.57 | convolution fusion | flops 3289251840 | bytes 33030152 | tf_op jit(solution)/shard_map/dot_general | solution.py:84
  199.1 3.3 collective-permute-start.10
  202.4 17.2 %collective-permute-done.10 = bf16[1792,128]{1,0:T(8,128)(2,1)S(1)} collective-permute-done((bf16[1792,128]{1,0:T(8,128)(2,1)S(1)}, bf16[1792,128]{1,0:T(8,128)(2,1)S(1)}, u32[]{:S(2)}, u32[]{:S(2)}) %collective-permute-start.10) | collective-permute-done | bytes 458784 | tf_op jit(solution)/shard_map/ppermute | solution.py:74
  220.7 8.4 %collective-permute-done.9 = bf16[1792,128]{1,0:T(8,128)(2,1)S(1)} collective-permute-done((bf16[1792,128]{1,0:T(8,128)(2,1)S(1)}, bf16[1792,128]{1,0:T(8,128)(2,1)S(1)}, u32[]{:S(2)}, u32[]{:S(2)}) %collective-permute-start.9) | collective-permute-done | bytes 458784 | tf_op jit(solution)/shard_map/ppermute | solution.py:69
  229.1 2.4 collective-permute-start.11
  231.7 2.5 collective-permute-done.12
  234.2 17.2 %collective-permute-done.11 = bf16[1792,128]{1,0:T(8,128)(2,1)S(1)} collective-permute-done((bf16[1792,128]{1,0:T(8,128)(2,1)S(1)}, bf16[1792,128]{1,0:T(8,128)(2,1)S(1)}, u32[]{:S(2)}, u32[]{:S(2)}) %collective-permute-start.11) | collective-permute-done | bytes 458784 | tf_op jit(solution)/shard_map/ppermute | solution.py:69
  251.3 2.5 collective-permute-start.13
  253.9 11.7 %collective-permute-done.13 = bf16[1792,128]{1,0:T(8,128)(2,1)S(1)} collective-permute-done((bf16[1792,128]{1,0:T(8,128)(2,1)S(1)}, bf16[1792,128]{1,0:T(8,128)(2,1)S(1)}, u32[]{:S(2)}, u32[]{:S(2)}) %collective-permute-start.13) | collective-permute-done | bytes 458784 | tf_op jit(solution)/shard_map/ppermute | solution.py:69
  265.7 13.3 %collective-permute-done.15 = bf16[1792,128]{1,0:T(8,128)(2,1)S(1)} collective-permute-done((bf16[1792,128]{1,0:T(8,128)(2,1)S(1)}, bf16[1792,128]{1,0:T(8,128)(2,1)S(1)}, u32[]{:S(2)}, u32[]{:S(2)}) %collective-permute-start.15) | collective-permute-done | bytes 458784 | tf_op jit(solution)/shard_map/ppermute | solution.py:69
  279.3 24.7 %select_reduce_fusion = f32[]{:T(128)} fusion(bf16[1792,7168]{1,0:T(8,128)(2,1)} %param.4, s32[1792]{0:T(1024)S(1)} %get-tuple-element.22), kind=kLoop, calls=%fused_computation | loop fusion | flops 51380224 | bytes 25697284 | tf_op jit(solution)/shard_map/reduce_sum | solution.py:50
  304.0 12.8 %convolution_bitcast_fusion = f32[1792,128]{1,0:T(8,128)} fusion(bf16[1792,7168]{1,0:T(8,128)(2,1)} %param.4, bf16[7168,128]{1,0:T(8,128)(2,1)S(1)} %collective-permute-done.16), kind=kOutput, calls=%fused_computation.4 | convolution fusion | flops 3288334336 | bytes 28442624 | tf_op jit(solution)/shard_map/dot_general | solution.py:85
  319.9 64.7 %all-reduce.5.cloned.1.call-done = f32[128,128]{0,1:T(8,128)} async-done(((f32[128,128]{0,1:T(8,128)}), f32[128,128]{0,1:T(8,128)}) %all-reduce.5.cloned.1.call-update) | async-done | bytes 65552 | tf_op jit(solution)/shard_map/psum | solution.py:57
  387.2 14.0 %multiply_reduce_fusion.3 = (f32[]{:T(128)}, f32[]{:T(128)}, f32[]{:T(128)}, f32[1792,128]{1,0:T(8,128)}) fusion(f32[1792,128]{1,0:T(8,128)S(1)} %get-tuple-element.10, f32[1792,128]{1,0:T(8,128)S(1)} %get-tuple-element.18, f32[1792,128]{1,0:T(8,128)S(1)} %fusion.1, f32[1792,128]{1,0:T(8,128)} %collective-permute-done.17, bf16[1792,7168]{1,0:T(8,128)(2,1)} %param.4, ...), kind=kOutput, calls=%fused_computation.22 | convolution fusion | flops 3290398720 | bytes 32112656 | tf_op jit(solution)/shard_map/dot_general | solution.py:84
  401.1 1.9 pad_maximum_fusion
  403.0 30.3 %psum.23 = f32[4]{0:T(128)S(1)} all-reduce(f32[4]{0:T(128)S(1)} %pad_maximum_fusion), channel_id=1, replica_groups=mesh['groups'=2,'row'=8,'col'=2] {'row','col'}, use_global_device_ids=true, to_apply=%region_7.8 | all-reduce | flops 4 | bytes 32 | tf_op jit(solution)/shard_map/psum | solution.py:97
  440.3 2.6 multiply_subtract_fusion
  (58 shorter events, 17.7 us)
Async XLA Ops:
  6.5 4.2 copy-start.4
  6.5 176.0 %all-reduce.3.cloned.1.call-start = ((), (), s32[]{:S(2)}) async-start(), calls=%async_computation | async-start | bytes 131072 | tf_op jit(solution)/shard_map/psum | solution.py:57
  12.4 23.3 %collective-permute-start.1 = (bf16[1792,128]{1,0:T(8,128)(2,1)S(1)}, bf16[1792,128]{1,0:T(8,128)(2,1)S(1)}, u32[]{:S(2)}, u32[]{:S(2)}) collective-permute-start(bf16[1792,128]{1,0:T(8,128)(2,1)S(1)} %get-tuple-element.12), channel_id=1, source_target_pairs={{0,14},{2,0},{4,2},{6,4},{8,6},{10,8},{12,10},{14,12},{1,15},{3,1}... | collective-permute-start | bytes 1376264 | tf_op jit(solution)/shard_map/ppermute | solution.py:74
  18.5 20.1 %collective-permute-start = (bf16[1792,128]{1,0:T(8,128)(2,1)S(1)}, bf16[1792,128]{1,0:T(8,128)(2,1)S(1)}, u32[]{:S(2)}, u32[]{:S(2)}) collective-permute-start(bf16[1792,128]{1,0:T(8,128)(2,1)S(1)} %get-tuple-element.12), channel_id=1, source_target_pairs={{0,2},{2,4},{4,6},{6,8},{8,10},{10,12},{12,14},{14,0},{1,3},{3,5},... | collective-permute-start | bytes 1376264 | tf_op jit(solution)/shard_map/ppermute | solution.py:69
  35.8 21.5 %collective-permute-start.3 = (bf16[1792,128]{1,0:T(8,128)(2,1)S(1)}, bf16[1792,128]{1,0:T(8,128)(2,1)S(1)}, u32[]{:S(2)}, u32[]{:S(2)}) collective-permute-start(bf16[1792,128]{1,0:T(8,128)(2,1)S(1)} %collective-permute-done.1), channel_id=1, source_target_pairs={{0,14},{2,0},{4,2},{6,4},{8,6},{10,8},{12,10},{14,12},{1,15},{3,1}... | collective-permute-start | bytes 1376264 | tf_op jit(solution)/shard_map/ppermute | solution.py:74
  38.6 21.2 %collective-permute-start.2 = (bf16[1792,128]{1,0:T(8,128)(2,1)S(1)}, bf16[1792,128]{1,0:T(8,128)(2,1)S(1)}, u32[]{:S(2)}, u32[]{:S(2)}) collective-permute-start(bf16[1792,128]{1,0:T(8,128)(2,1)S(1)} %collective-permute-done), channel_id=1, source_target_pairs={{0,2},{2,4},{4,6},{6,8},{8,10},{10,12},{12,14},{14,0},{1,3},{3,5},... | collective-permute-start | bytes 1376264 | tf_op jit(solution)/shard_map/ppermute | solution.py:69
  57.3 22.8 %collective-permute-start.5 = (bf16[1792,128]{1,0:T(8,128)(2,1)S(1)}, bf16[1792,128]{1,0:T(8,128)(2,1)S(1)}, u32[]{:S(2)}, u32[]{:S(2)}) collective-permute-start(bf16[1792,128]{1,0:T(8,128)(2,1)S(1)} %collective-permute-done.3), channel_id=1, source_target_pairs={{0,14},{2,0},{4,2},{6,4},{8,6},{10,8},{12,10},{14,12},{1,15},{3,1}... | collective-permute-start | bytes 1376264 | tf_op jit(solution)/shard_map/ppermute | solution.py:74
  59.8 16.9 %collective-permute-start.4 = (bf16[1792,128]{1,0:T(8,128)(2,1)S(1)}, bf16[1792,128]{1,0:T(8,128)(2,1)S(1)}, u32[]{:S(2)}, u32[]{:S(2)}) collective-permute-start(bf16[1792,128]{1,0:T(8,128)(2,1)S(1)} %collective-permute-done.2), channel_id=1, source_target_pairs={{0,2},{2,4},{4,6},{6,8},{8,10},{10,12},{12,14},{14,0},{1,3},{3,5},... | collective-permute-start | bytes 1376264 | tf_op jit(solution)/shard_map/ppermute | solution.py:69
  76.8 17.7 %collective-permute-start.6 = (bf16[1792,128]{1,0:T(8,128)(2,1)S(1)}, bf16[1792,128]{1,0:T(8,128)(2,1)S(1)}, u32[]{:S(2)}, u32[]{:S(2)}) collective-permute-start(bf16[1792,128]{1,0:T(8,128)(2,1)S(1)} %collective-permute-done.4), channel_id=1, source_target_pairs={{0,2},{2,4},{4,6},{6,8},{8,10},{10,12},{12,14},{14,0},{1,3},{3,5},... | collective-permute-start | bytes 1376264 | tf_op jit(solution)/shard_map/ppermute | solution.py:69
  96.9 16.8 %copy-start = (bf16[128,1792]{1,0:T(8,128)(2,1)S(1)}, bf16[128,1792]{1,0:T(8,128)(2,1)}, u32[]{:S(2)}) copy-start(bf16[128,1792]{1,0:T(8,128)(2,1)} %param.5) | copy-start | bytes 1376260
  96.9 3.9 collective-permute-start.7
  113.5 71.5 %collective-permute-start.8 = (f32[1792,128]{1,0:T(8,128)}, f32[1792,128]{1,0:T(8,128)S(1)}, u32[]{:S(2)}, u32[]{:S(2)}) collective-permute-start(f32[1792,128]{1,0:T(8,128)} %convolution_bitcast_fusion.2), channel_id=1, source_target_pairs={{0,1},{1,0},{2,3},{3,2},{4,5},{5,4},{6,7},{7,6},{8,9},{9,8},{10,11... | collective-permute-start | bytes 2752520 | tf_op jit(solution)/shard_map/ppermute | solution.py:13
  114.6 269.9 %all-reduce.5.cloned.1.call-start = ((), (), s32[]{:S(2)}) async-start(), calls=%async_computation.1 | async-start | bytes 131072 | tf_op jit(solution)/shard_map/psum | solution.py:57
  185.0 0.9 copy-start.3
  199.1 20.6 %collective-permute-start.10 = (bf16[1792,128]{1,0:T(8,128)(2,1)S(1)}, bf16[1792,128]{1,0:T(8,128)(2,1)S(1)}, u32[]{:S(2)}, u32[]{:S(2)}) collective-permute-start(bf16[1792,128]{1,0:T(8,128)(2,1)S(1)} %get-tuple-element.9), channel_id=1, source_target_pairs={{0,14},{2,0},{4,2},{6,4},{8,6},{10,8},{12,10},{14,12},{1,15},{3,1}... | collective-permute-start | bytes 1376264 | tf_op jit(solution)/shard_map/ppermute | solution.py:74
  202.4 26.7 %collective-permute-start.9 = (bf16[1792,128]{1,0:T(8,128)(2,1)S(1)}, bf16[1792,128]{1,0:T(8,128)(2,1)S(1)}, u32[]{:S(2)}, u32[]{:S(2)}) collective-permute-start(bf16[1792,128]{1,0:T(8,128)(2,1)S(1)} %get-tuple-element.9), channel_id=1, source_target_pairs={{0,2},{2,4},{4,6},{6,8},{8,10},{10,12},{12,14},{14,0},{1,3},{3,5},... | collective-permute-start | bytes 1376264 | tf_op jit(solution)/shard_map/ppermute | solution.py:69
  219.6 14.5 %collective-permute-start.12 = (bf16[1792,128]{1,0:T(8,128)(2,1)S(1)}, bf16[1792,128]{1,0:T(8,128)(2,1)S(1)}, u32[]{:S(2)}, u32[]{:S(2)}) collective-permute-start(bf16[1792,128]{1,0:T(8,128)(2,1)S(1)} %collective-permute-done.10), channel_id=1, source_target_pairs={{0,14},{2,0},{4,2},{6,4},{8,6},{10,8},{12,10},{14,12},{1,15},{3,1}... | collective-permute-start | bytes 1376264 | tf_op jit(solution)/shard_map/ppermute | solution.py:74
  229.1 22.2 %collective-permute-start.11 = (bf16[1792,128]{1,0:T(8,128)(2,1)S(1)}, bf16[1792,128]{1,0:T(8,128)(2,1)S(1)}, u32[]{:S(2)}, u32[]{:S(2)}) collective-permute-start(bf16[1792,128]{1,0:T(8,128)(2,1)S(1)} %collective-permute-done.9), channel_id=1, source_target_pairs={{0,2},{2,4},{4,6},{6,8},{8,10},{10,12},{12,14},{14,0},{1,3},{3,5},... | collective-permute-start | bytes 1376264 | tf_op jit(solution)/shard_map/ppermute | solution.py:69
  234.2 31.5 %collective-permute-start.14 = (bf16[1792,128]{1,0:T(8,128)(2,1)S(1)}, bf16[1792,128]{1,0:T(8,128)(2,1)S(1)}, u32[]{:S(2)}, u32[]{:S(2)}) collective-permute-start(bf16[1792,128]{1,0:T(8,128)(2,1)S(1)} %collective-permute-done.12), channel_id=1, source_target_pairs={{0,14},{2,0},{4,2},{6,4},{8,6},{10,8},{12,10},{14,12},{1,15},{3,1}... | collective-permute-start | bytes 1376264 | tf_op jit(solution)/shard_map/ppermute | solution.py:74
  251.3 14.3 %collective-permute-start.13 = (bf16[1792,128]{1,0:T(8,128)(2,1)S(1)}, bf16[1792,128]{1,0:T(8,128)(2,1)S(1)}, u32[]{:S(2)}, u32[]{:S(2)}) collective-permute-start(bf16[1792,128]{1,0:T(8,128)(2,1)S(1)} %collective-permute-done.11), channel_id=1, source_target_pairs={{0,2},{2,4},{4,6},{6,8},{8,10},{10,12},{12,14},{14,0},{1,3},{3,5},... | collective-permute-start | bytes 1376264 | tf_op jit(solution)/shard_map/ppermute | solution.py:69
  265.6 13.4 %collective-permute-start.15 = (bf16[1792,128]{1,0:T(8,128)(2,1)S(1)}, bf16[1792,128]{1,0:T(8,128)(2,1)S(1)}, u32[]{:S(2)}, u32[]{:S(2)}) collective-permute-start(bf16[1792,128]{1,0:T(8,128)(2,1)S(1)} %collective-permute-done.13), channel_id=1, source_target_pairs={{0,2},{2,4},{4,6},{6,8},{8,10},{10,12},{12,14},{14,0},{1,3},{3,5},... | collective-permute-start | bytes 1376264 | tf_op jit(solution)/shard_map/ppermute | solution.py:69
  279.1 24.9 %copy-start.1 = (bf16[14336,128]{1,0:T(8,128)(2,1)}, bf16[14336,128]{1,0:T(8,128)(2,1)S(1)}, u32[]{:S(2)}) copy-start(bf16[14336,128]{1,0:T(8,128)(2,1)S(1)} %constant_dynamic-update-slice_fusion) | copy-start | bytes 11010052
  279.2 24.7 %collective-permute-start.16 = (bf16[7168,128]{1,0:T(8,128)(2,1)S(1)}, bf16[7168,128]{1,0:T(8,128)(2,1)S(1)}, u32[]{:S(2)}, u32[]{:S(2)}) collective-permute-start(bf16[7168,128]{1,0:T(8,128)(2,1)S(1)} %constant_dynamic-slice_fusion), channel_id=1, source_target_pairs={{0,1},{1,0},{2,3},{3,2},{4,5},{5,4},{6,7},{7,6},{8,9},{9,8},{10,11... | collective-permute-start | bytes 5505032 | tf_op jit(solution)/shard_map/ppermute | solution.py:13
  316.7 70.4 %collective-permute-start.17 = (f32[1792,128]{1,0:T(8,128)}, f32[1792,128]{1,0:T(8,128)}, u32[]{:S(2)}, u32[]{:S(2)}) collective-permute-start(f32[1792,128]{1,0:T(8,128)} %convolution_bitcast_fusion), channel_id=1, source_target_pairs={{0,1},{1,0},{2,3},{3,2},{4,5},{5,4},{6,7},{7,6},{8,9},{9,8},{10,11... | collective-permute-start | bytes 2752520 | tf_op jit(solution)/shard_map/ppermute | solution.py:13
  384.6 2.6 copy-start.2
Sparse Core Ops, SparseCore 0:
  114.7 67.7 all-reduce.2
  317.9 66.6 all-reduce.4
